TPU v7x, 32 devices: a whole 2x2x4 slice. The times are simulated.
32 devices in a mesh: fsdp: 8 (over z, x), pipe: 2 (over core), dp: 2 (over y).
Axes of the slice: x: 2, y: 2, z: 4, core: 2. Of those that a mesh axis runs over, the one named last changes fastest.
Arguments:
- video_tokens: bfloat16 [2, 1024, 2560], P('dp', 'fsdp'), may hold values from -6 to 6
- cached_out: bfloat16 [2, 2, 1024, 2560], P('pipe', 'dp', 'fsdp'), may hold values from -6 to 6
- fresh_mask: int32 [2, 2, 1024], P('pipe', 'dp', 'fsdp'), may hold values from 0 to 1, as said below
- timestep: int32 [2], P('dp'), may hold values from 0 to 49
- up_weight: bfloat16 [2, 7168, 2560], P('pipe', 'fsdp'), may hold values from -0.125 to 0.125
- down_weight: bfloat16 [2, 7168, 2560], P('pipe', 'fsdp'), may hold values from -0.0625 to 0.0625
- router_in: bfloat16 [2, 2560, 256], P('pipe', 'fsdp'), may hold values from -0.125 to 0.125
- router_bias: float32 [2, 50, 256], P('pipe'), may hold values from -6 to 6
- router_out: float32 [2, 256], P('pipe'), may hold values from -0.375 to 0.375
- out_cotangent: bfloat16 [2, 1024, 2560], P('dp', 'fsdp'), may hold values from -0.119628906 to 0.119628906
Outputs:
- blended: bfloat16 [2, 2, 1024, 2560], P('pipe', 'dp', 'fsdp')
- grad_router_in: float32 [2, 2560, 256], P('pipe', 'fsdp')
- grad_router_bias: float32 [2, 50, 256], P('pipe')
- grad_router_out: float32 [2, 256], P('pipe')
Inputs may be any that keep to these rules, and one draw needn't show every extreme that they name: `fresh_mask`: for each section and video, the 128 consecutive tokens of one index of fsdp hold 1 to 2 ones, and some index holds exactly 2.
All inputs are finite; a program needn't handle non-finite values.
Results may differ from a plain program's by a relative error of at most 0.023.
Values may be sent and summed in bfloat16 or wider, within the bound.
A program may use at most 64 MiB of HBM per device.

v0:
```python
import jax
import jax.numpy as jnp
from jax import lax
from jax.sharding import PartitionSpec as P

FRESH = 2


layer_eps = 1e-06
gelu_scale = 0.7978845608028654
gelu_cubic = 0.044715


def from_behind(block, axis, distance):
    devices = range(lax.axis_size(axis))
    route = [(i - distance, i) for i in devices if i - distance in devices]
    return lax.ppermute(block, axis, route)


def for_sending(value):
    return jax.tree.map(lambda a: a.astype(jnp.bfloat16) if a.dtype == jnp.float32 else a, value)


def gelu_tanh(values):
    inner_arg = gelu_scale * (values + gelu_cubic * values * values * values)
    return 0.5 * values * (1.0 + jnp.tanh(inner_arg))


def gelu_slope(values):
    inner_arg = gelu_scale * (values + gelu_cubic * values * values * values)
    tanh_val = jnp.tanh(inner_arg)
    return 0.5 * (1.0 + tanh_val) + 0.5 * values * (1.0 - tanh_val * tanh_val) * gelu_scale * (
        1.0 + 3.0 * gelu_cubic * values * values
    )


def normalize(inputs):
    values = inputs.astype(jnp.float32)
    center = values - jnp.mean(values, axis=1, keepdims=True)
    inv_std = lax.rsqrt(jnp.mean(center * center, axis=1, keepdims=True) + layer_eps)
    return (center * inv_std, inv_std)


def normalize_back(scaled, inv_std, grads):
    return inv_std * (
        grads
        - jnp.mean(grads, axis=1, keepdims=True)
        - scaled * jnp.mean(grads * scaled, axis=1, keepdims=True)
    )


def contract_last(left, right):
    return lax.dot_general(
        left, right, (((1,), (1,)), ((), ())), preferred_element_type=jnp.float32
    )


def contract_first(left, right):
    return lax.dot_general(
        left, right, (((0,), (0,)), ((), ())), preferred_element_type=jnp.float32
    )


def gather_gate(gate_grad):
    return lax.all_gather(gate_grad, "fsdp", axis=0, tiled=True)


def body(
    video_tokens,
    cached_out,
    fresh_mask,
    timestep,
    up_weight,
    down_weight,
    router_in,
    router_bias,
    router_out,
    out_cotangent,
):
    section_id = lax.axis_index("pipe")
    column_slot = lax.axis_index("fsdp")
    inputs_first = video_tokens[0]
    cached = cached_out[0, 0]
    mask_row = fresh_mask[0, 0]
    w_up = up_weight[0]
    w_down = down_weight[0]
    r_in = router_in[0]
    r_out = router_out[0]
    tok_rows = inputs_first.shape[0]
    shard_cols = r_in.shape[0]
    hot_step = (jnp.arange(router_bias.shape[1]) == timestep[0]).astype(jnp.float32)
    bias_row = jnp.dot(hot_step, router_bias[0], precision=lax.Precision.HIGHEST)
    picked = jnp.argsort(1 - mask_row, stable=True)[:FRESH]
    live_rows = (jnp.arange(FRESH) < jnp.sum(mask_row)).astype(jnp.float32)

    def select(values):
        return jnp.take(values, picked, axis=0)

    def spread(values):
        return jnp.zeros((tok_rows, values.shape[1]), values.dtype).at[picked].add(values)

    def forward(inputs):
        rows_in = select(inputs)
        rows_cached = select(cached).astype(jnp.float32)
        scaled, inv_std = normalize(rows_in)
        normed = scaled.astype(jnp.bfloat16)
        row_count = normed.shape[0]
        gathered = lax.all_gather(normed, "fsdp", axis=0, tiled=True)
        pre_act = contract_last(gathered, w_up)
        hid_act = gelu_tanh(pre_act).astype(jnp.bfloat16)
        block_sum = lax.psum_scatter(
            jnp.dot(hid_act, w_down, preferred_element_type=jnp.float32).astype(jnp.bfloat16),
            "fsdp",
            scatter_dimension=0,
            tiled=True,
        ).astype(jnp.float32)
        columns = lax.dynamic_slice_in_dim(gathered, column_slot * shard_cols, shard_cols, 1)
        router_part = jnp.dot(columns, r_in, preferred_element_type=jnp.float32)
        router_pre = (
            lax.psum(router_part.astype(jnp.bfloat16), "fsdp").astype(jnp.float32)
            + bias_row[None, :]
        )
        gate_all = jax.nn.sigmoid(
            jnp.dot(gelu_tanh(router_pre), r_out, precision=lax.Precision.HIGHEST)
        )
        gate_own = lax.dynamic_slice_in_dim(gate_all, column_slot * row_count, row_count, 0)
        fresh_out = rows_in.astype(jnp.float32) + block_sum
        delta_rows = live_rows[:, None] * gate_own[:, None] * (fresh_out - rows_cached)
        blended = (cached.astype(jnp.float32) + spread(delta_rows)).astype(jnp.bfloat16)
        stored = (
            scaled,
            inv_std,
            columns,
            pre_act,
            router_pre,
            gate_all,
            gate_own,
            fresh_out,
            rows_cached,
        )
        return (blended, stored)

    def local_grads(stored, cot_rows):
        gate_own = stored[6]
        fresh_out = stored[7]
        rows_cached = stored[8]
        gate_grad = jnp.sum(cot_rows * live_rows[:, None] * (fresh_out - rows_cached), axis=1)
        fresh_grad = cot_rows * (live_rows * gate_own)[:, None]
        return (gate_grad, fresh_grad)

    def router_grads(stored, gate_all_grad):
        columns = stored[2]
        router_pre = stored[4]
        gate_all = stored[5]
        logit_grad = gate_all_grad * gate_all * (1.0 - gate_all)
        out_grad = jnp.dot(logit_grad, gelu_tanh(router_pre), precision=lax.Precision.HIGHEST)
        hidden_grad = logit_grad[:, None] * r_out[None, :] * gelu_slope(router_pre)
        hidden_b = hidden_grad.astype(jnp.bfloat16)
        in_grad = contract_first(columns, hidden_b)
        bias_grad = hot_step[:, None] * jnp.sum(hidden_grad, axis=0)[None, :]
        return (hidden_b, (in_grad, bias_grad, out_grad))

    blended_first, stored_first = forward(inputs_first)
    arriving = from_behind(blended_first, "pipe", 1)
    inputs_second = jnp.where(section_id == 1, arriving, inputs_first)
    blended_out, stored = forward(inputs_second)
    cot_second = select(out_cotangent[0]).astype(jnp.float32)
    gate_grad, fresh_grad = local_grads(stored, cot_second)
    hidden_b, grads_second = router_grads(stored, gather_gate(gate_grad))
    fresh_rows = lax.all_gather(fresh_grad.astype(jnp.bfloat16), "fsdp", axis=0, tiled=True)
    act_grad = contract_last(fresh_rows, w_down)
    pre_grad = (act_grad * gelu_slope(stored[3])).astype(jnp.bfloat16)
    row_count = fresh_grad.shape[0]
    total_rows = jnp.dot(pre_grad, w_up, preferred_element_type=jnp.float32)
    router_term = contract_last(hidden_b, r_in)
    current = lax.dynamic_slice_in_dim(total_rows, column_slot * shard_cols, shard_cols, 1)
    normed_grad = lax.psum_scatter(
        lax.dynamic_update_slice_in_dim(
            total_rows, current + router_term, column_slot * shard_cols, 1
        ).astype(jnp.bfloat16),
        "fsdp",
        scatter_dimension=0,
        tiled=True,
    ).astype(jnp.float32)
    input_grad = fresh_grad + normalize_back(stored[0], stored[1], normed_grad)
    positions = picked.astype(jnp.float32)
    got_rows, got_positions = from_behind((input_grad, positions), "pipe", -1)
    returning = (
        jnp.zeros((tok_rows, input_grad.shape[1]), jnp.float32)
        .at[got_positions.astype(jnp.int32)]
        .add(got_rows)
    )
    gate_grad_first, unused_grad = local_grads(stored, select(returning))
    unused_hidden, grads_first = router_grads(stored, gather_gate(gate_grad_first))
    chosen = tuple(
        (
            jnp.where(section_id == 1, second_grad, first_grad)
            for second_grad, first_grad in zip(grads_second, grads_first)
        )
    )
    summed = jax.tree.map(
        lambda part: part.astype(jnp.float32), lax.psum(for_sending(chosen), "dp")
    )
    return (blended_out[None, None], summed[0][None], summed[1][None], summed[2][None])


def solution(mesh):
    placed = (
        P("dp", "fsdp", None),
        P("pipe", "dp", "fsdp", None),
        P("pipe", "dp", "fsdp"),
        P("dp"),
        P("pipe", "fsdp", None),
        P("pipe", "fsdp", None),
        P("pipe", "fsdp", None),
        P("pipe", None, None),
        P("pipe", None),
        P("dp", "fsdp", None),
    )
    return jax.shard_map(
        body,
        mesh=mesh,
        in_specs=placed,
        out_specs=(
            P("pipe", "dp", "fsdp", None),
            P("pipe", "fsdp", None),
            P("pipe", None, None),
            P("pipe", None),
        ),
        check_vma=False,
    )
```

profile of v0, /device:TPU:0, one launch (start us, length us, event | category | flops | bytes accessed | tf_op | source)
XLA Modules:
  0.0 421.7 jit_solution(18369744704275985153)
XLA Ops:
  7.2 1.3 fusion.193
  8.6 2.5 sort.17
  11.1 1.8 gather_fusion.1
  13.4 32.4 %all-gather = bf16[8,2,2560]{2,1,0:T(2,128)(2,1)S(1)} all-gather(bf16[1,2,2560]{2,1,0:T(2,128)(2,1)S(1)} %fusion.127), channel_id=1, replica_groups=mesh['fsdp'=8,'pipe'=2,'dp'=2] {'fsdp'}, dimensions={0}, use_global_device_ids=true | all-gather | bytes 92160 | tf_op jit(solution)/shard_map/all_gather | solution.py:108
  45.8 6.5 %fusion.12 = bf16[16,2560]{1,0:T(8,128)(2,1)} fusion(bf16[1,896,2560]{2,1,0:T(8,128)(2,1)} %param.17, bf16[16,2560]{1,0:T(8,128)(2,1)S(1)} %reshape.151, bf16[1,896,2560]{2,1,0:T(8,128)(2,1)} %param.16), kind=kOutput, calls=%fused_computation.20 | convolution fusion | flops 146970624 | bytes 9338880 | tf_op jit(solution)/shard_map/dot_general | solution.py:112
  52.7 21.6 %psum.35 = bf16[16,256]{1,0:T(8,128)(2,1)S(1)} all-reduce(bf16[16,256]{1,0:T(8,128)(2,1)S(1)} %convolution_convert_fusion.1), channel_id=1, replica_groups=mesh['fsdp'=8,'pipe'=2,'dp'=2] {'fsdp'}, use_global_device_ids=true, to_apply=%region_4.6 | all-reduce | flops 4096 | bytes 16384 | tf_op jit(solution)/shard_map/psum | solution.py:120
  78.0 45.0 %all-reduce.13.cloned.1.call-done = bf16[16,2560]{1,0:T(8,128)(2,1)} async-done(((bf16[16,2560]{1,0:T(8,128)(2,1)}), bf16[16,2560]{1,0:T(8,128)(2,1)}) %all-reduce.13.cloned.1.call-update) | async-done | bytes 81936
  123.0 1.4 scatter_custom_fusion
  125.3 1.3 collective-permute-start
  126.7 1.3 collective-permute-start.1
  129.8 1.2 broadcast_select_fusion
  132.1 30.5 %all-gather.1 = bf16[8,2,2560]{2,1,0:T(2,128)(2,1)S(1)} all-gather(bf16[1,2,2560]{2,1,0:T(2,128)(2,1)S(1)} %fusion.126), channel_id=1, replica_groups=mesh['fsdp'=8,'pipe'=2,'dp'=2] {'fsdp'}, dimensions={0}, use_global_device_ids=true | all-gather | bytes 92160 | tf_op jit(solution)/shard_map/all_gather | solution.py:108
  162.7 3.6 fusion.8
  166.5 3.7 fusion.15
  170.2 20.5 %psum.36 = bf16[16,256]{1,0:T(8,128)(2,1)S(1)} all-reduce(bf16[16,256]{1,0:T(8,128)(2,1)S(1)} %convolution_convert_fusion), channel_id=1, replica_groups=mesh['fsdp'=8,'pipe'=2,'dp'=2] {'fsdp'}, use_global_device_ids=true, to_apply=%region_9.11 | all-reduce | flops 4096 | bytes 16384 | tf_op jit(solution)/shard_map/psum | solution.py:120
  191.6 48.1 %all-reduce.15.cloned.1.call-done = bf16[16,2560]{1,0:T(8,128)(2,1)} async-done(((bf16[16,2560]{1,0:T(8,128)(2,1)}), bf16[16,2560]{1,0:T(8,128)(2,1)}) %all-reduce.15.cloned.1.call-update) | async-done | bytes 81936
  239.6 1.0 fusion.93
  240.6 30.5 %all-gather.2 = bf16[8,2,2560]{2,1,0:T(2,128)(2,1)S(1)} all-gather(bf16[1,2,2560]{2,1,0:T(2,128)(2,1)S(1)} %get-tuple-element.21), channel_id=1, replica_groups=mesh['fsdp'=8,'pipe'=2,'dp'=2] {'fsdp'}, dimensions={0}, use_global_device_ids=true | all-gather | bytes 92160 | tf_op jit(solution)/shard_map/all_gather | solution.py:170
  271.5 5.8 %fusion.6 = f32[16,2560]{1,0:T(8,128)S(1)} fusion(bf16[1,896,2560]{2,1,0:T(8,128)(2,1)} %param.16, bf16[16,2560]{1,0:T(8,128)(2,1)S(1)} %reshape.155, bf16[1,896,2560]{2,1,0:T(8,128)(2,1)} %param.17, f32[16,896]{1,0:T(8,128)S(1)} %fusion.8), kind=kOutput, calls=%fused_computation.14 | convolution fusion | flops 147073024 | bytes 9478144 | tf_op jit(solution)/shard_map/dot_general | solution.py:174
  277.3 20.1 %all-reduce = f32[16]{0:T(128)S(1)} all-reduce(f32[16]{0:T(128)S(1)} %dynamic-update-slice), channel_id=1, replica_groups=mesh['fsdp'=8,'pipe'=2,'dp'=2] {'fsdp'}, use_global_device_ids=true, to_apply=%add | all-reduce | flops 16 | bytes 128
  298.7 1.2 scatter_custom_fusion.1
  299.9 0.9 convert_bitcast_fusion
  300.8 64.7 %all-reduce.17.cloned.1.call-done = bf16[16,2560]{1,0:T(8,128)(2,1)} async-done(((bf16[16,2560]{1,0:T(8,128)(2,1)}), bf16[16,2560]{1,0:T(8,128)(2,1)}) %all-reduce.17.cloned.1.call-update) | async-done | bytes 81936
  365.6 1.0 convert_reduce_fusion
  367.5 1.3 collective-permute-start.2
  369.1 1.5 collective-permute-done.2
  370.5 1.0 scatter_custom_fusion.2
  372.7 20.2 %all-reduce.1 = f32[16]{0:T(128)S(1)} all-reduce(f32[16]{0:T(128)S(1)} %dynamic-update-slice.1), channel_id=1, replica_groups=mesh['fsdp'=8,'pipe'=2,'dp'=2] {'fsdp'}, use_global_device_ids=true, to_apply=%add.1 | all-reduce | flops 16 | bytes 128
  393.1 1.0 fusion.19
  394.2 8.9 %all-reduce.5 = (bf16[1,50,256]{2,0,1:T(2,128)(2,1)S(1)}, bf16[1,256]{1,0:T(2,128)(2,1)S(1)}) all-reduce(bf16[1,50,256]{2,0,1:T(2,128)(2,1)S(1)} %broadcast_in_dim.75, bf16[1,256]{1,0:T(2,128)(2,1)S(1)} %broadcast_in_dim.77), channel_id=1, replica_groups=mesh['fsdp'=8,'pipe'=2,'dp'=2] {'dp'}, use_global_device_ids=true, to_apply=%region_21.23 | all-reduce | flops 13056 | bytes 52224 | tf_op jit(solution)/shard_map/psum | solution.py:202
  404.4 9.1 %all-reduce.11.cloned.1.call-done = bf16[1,320,256]{2,1,0:T(8,128)(2,1)} async-done(((bf16[1,320,256]{2,1,0:T(8,128)(2,1)}), bf16[1,320,256]{2,1,0:T(8,128)(2,1)}) %all-reduce.11.cloned.1.call-update) | async-done | bytes 163856 | tf_op jit(solution)/shard_map/psum | solution.py:202
  413.5 1.7 broadcast_in_dim.74
  (79 shorter events, 13.2 us)
Async XLA Ops:
  7.2 120.8 %copy-start = (bf16[1,128,2560]{2,1,0:T(8,128)(2,1)S(1)}, bf16[1,128,2560]{2,1,0:T(8,128)(2,1)}, u32[]{:S(2)}) copy-start(bf16[1,128,2560]{2,1,0:T(8,128)(2,1)} %param.21) | copy-start | bytes 1966084
  7.2 115.8 %all-reduce.13.cloned.1.call-start = ((), (), s32[]{:S(2)}) async-start(), calls=%async_computation.1 | async-start | bytes 163840
  45.8 6.6 %copy-start.1 = (bf16[1,320,256]{2,1,0:T(8,128)(2,1)S(1)}, bf16[1,320,256]{2,1,0:T(8,128)(2,1)}, u32[]{:S(2)}) copy-start(bf16[1,320,256]{2,1,0:T(8,128)(2,1)} %param.18) | copy-start | bytes 491524
  45.8 29.1 %copy-start.2 = (bf16[1,1,128,2560]{3,2,1,0:T(8,128)(2,1)S(1)}, bf16[1,1,128,2560]{3,2,1,0:T(8,128)(2,1)}, u32[]{:S(2)}) copy-start(bf16[1,1,128,2560]{3,2,1,0:T(8,128)(2,1)} %param.13) | copy-start | bytes 1966084
  52.3 23.4 %copy-start.3 = (f32[1,50,256]{2,0,1:T(1,128)S(1)}, f32[1,50,256]{2,0,1:T(1,128)}, u32[]{:S(2)}) copy-start(f32[1,50,256]{2,0,1:T(1,128)} %param.19) | copy-start | bytes 153604
  52.4 23.5 %copy-start.5 = (u32[32]{0:T(128)S(1)}, u32[32]{0:T(128)}, u32[]{:S(2)}) copy-start(u32[32]{0:T(128)} %constant.94) | copy-start | bytes 388
  52.4 24.8 %copy-start.4 = (f32[1,256]{1,0:T(1,128)S(1)}, f32[1,256]{1,0:T(1,128)}, u32[]{:S(2)}) copy-start(f32[1,256]{1,0:T(1,128)} %param.20) | copy-start | bytes 3076
  52.4 187.3 %all-reduce.15.cloned.1.call-start = ((), (), s32[]{:S(2)}) async-start(), calls=%async_computation.2 | async-start | bytes 163840
  125.3 4.5 %collective-permute-start = (bf16[128,2560]{1,0:T(8,128)(2,1)}, bf16[128,2560]{1,0:T(8,128)(2,1)S(1)}, u32[]{:S(2)}, u32[]{:S(2)}) collective-permute-start(bf16[128,2560]{1,0:T(8,128)(2,1)} %convert_element_type.120), channel_id=1, source_target_pairs={{0,2},{1,3},{4,6},{5,7},{8,10},{9,11},{12,14},{13,15},{16,18},{17,... | collective-permute-start | bytes 1966088 | tf_op jit(solution)/shard_map/ppermute | solution.py:17
  126.7 3.1 collective-permute-start.1
  170.2 195.4 %all-reduce.17.cloned.1.call-start = ((), (), s32[]{:S(2)}) async-start(), calls=%async_computation.3 | async-start | bytes 163840
  298.6 114.8 %all-reduce.11.cloned.1.call-start = ((), (), s32[]{:S(2)}) async-start(), calls=%async_computation | async-start | bytes 327680 | tf_op jit(solution)/shard_map/psum | solution.py:202
  367.5 3.1 collective-permute-start.2
Sparse Core Ops, SparseCore 0:
  52.5 70.4 all-reduce.12
  170.3 69.3 all-reduce.14
  298.8 66.7 all-reduce.16
  394.2 19.2 all-reduce.10
where the time goes:
time: 422 us
  blocking collectives  185 us (44%)
  waiting for transfers between devices  168 us (40%)
  matrix products  22.2 us (5%)
  other arithmetic  20.6 us (5%)
  between operations  16 us (4%)
  local copies, waits for them, and re-layouts  5.75 us (1%)
    unnamed x7, waiting for transfers between devices  158 us
    all_gather x2, blocking collectives, forward(): gathered = lax.all_gather(normed, 'fsdp', axis=0, tiled=True)  62.9 us
    psum x2, blocking collectives, forward(): lax.psum(router_part.astype(jnp.bfloat16), 'fsdp').astype(jnp.float32)  42.1 us
    unnamed x2, blocking collectives  40.3 us
    all_gather x1, blocking collectives, body(): lax.all_gather(fresh_grad.astype(jnp.bfloat16), 'fsdp', axis=0, tiled=True)  30.5 us
    dot_general x2, matrix products, forward(): jnp.dot(hid_act, w_down, preferred_element_type=jnp.float32)  10.2 us
    psum x1, waiting for transfers between devices, body(): lax.psum(for_sending(chosen), 'dp')  9.1 us
    psum x1, blocking collectives, body(): lax.psum(for_sending(chosen), 'dp')  8.92 us
  transfers between devices with their start and end apart: 7, of which 5 were waited for; matrix products, arithmetic and copies ran while one was open for 2% of the time, Pallas kernels for 0%

commit v1 on v0

v1 whole, which is shorter than its diff:
```python
import functools

import jax
import jax.numpy as jnp
from jax import lax
from jax.experimental import pallas as pl
from jax.experimental.pallas import tpu as pltpu
from jax.sharding import PartitionSpec as P

FRESH = 2

layer_eps = 1e-06
gelu_scale = 0.7978845608028654
gelu_cubic = 0.044715
F32 = jnp.float32
BF16 = jnp.bfloat16
MESH = pl.DeviceIdType.MESH


def gelu_both(values):
    inner_arg = gelu_scale * (values + gelu_cubic * values * values * values)
    tanh_val = jnp.tanh(inner_arg)
    gelu = 0.5 * values * (1.0 + tanh_val)
    slope = 0.5 * (1.0 + tanh_val) + 0.5 * values * (1.0 - tanh_val * tanh_val) * gelu_scale * (
        1.0 + 3.0 * gelu_cubic * values * values
    )
    return gelu, slope


def normalize(values):
    center = values - jnp.mean(values, axis=1, keepdims=True)
    inv_std = lax.rsqrt(jnp.mean(center * center, axis=1, keepdims=True) + layer_eps)
    return center * inv_std, inv_std


def normalize_back(scaled, inv_std, grads):
    return inv_std * (
        grads
        - jnp.mean(grads, axis=1, keepdims=True)
        - scaled * jnp.mean(grads * scaled, axis=1, keepdims=True)
    )


def dot_nn(left, right):
    return jnp.dot(left, right, preferred_element_type=F32)


def dot_nt(left, right):
    return lax.dot_general(left, right, (((1,), (1,)), ((), ())), preferred_element_type=F32)


def dot_tn(left, right):
    return lax.dot_general(left, right, (((0,), (0,)), ((), ())), preferred_element_type=F32)


def kernel(
    n,
    n_dp,
    tokens_hbm,
    cached_hbm,
    mask_ref,
    step_ref,
    up_hbm,
    down_hbm,
    rin_ref,
    bias_ref,
    rout_ref,
    cot_hbm,
    blended_hbm,
    in_grad_ref,
    bias_grad_ref,
    out_grad_ref,
    up,
    down,
    first,
    cached,
    blend,
    sel,
    psel,
    xin,
    in1,
    x32,
    pre,
    send1,
    recv1,
    delta,
    delta_in,
    factors,
    factors_in,
    fgrad,
    total,
    send2,
    recv2,
    cols,
    gmsg,
    gfirst,
    hid,
    load_sem,
    sel_sems,
    x_send,
    x_recv,
    r1_send,
    r1_recv,
    aux_sems,
    f_send,
    f_recv,
    r2_send,
    r2_recv,
    c_send,
    c_recv,
    g_send,
    g_recv,
    out_sem,
):
    k = lax.axis_index("fsdp")
    p = lax.axis_index("pipe")
    v = lax.axis_index("dp")
    is0 = p == 0
    is1 = p == 1
    dim = up.shape[1]
    rh = rin_ref.shape[1]
    cols_n = rin_ref.shape[0]
    rows = n * FRESH

    load_rows = pltpu.make_async_copy(tokens_hbm, first, load_sem.at[0])
    load_cot = pltpu.make_async_copy(cot_hbm, first, load_sem.at[0])
    load_cached = pltpu.make_async_copy(cached_hbm, cached, load_sem.at[1])
    load_up = pltpu.make_async_copy(up_hbm, up, load_sem.at[2])
    load_down = pltpu.make_async_copy(down_hbm, down, load_sem.at[3])

    @pl.when(is0)
    def _():
        load_rows.start()

    @pl.when(is1)
    def _():
        load_cot.start()

    load_cached.start()
    load_up.start()
    load_down.start()

    barrier = pltpu.get_barrier_semaphore()
    count = n * 2 * n_dp
    flat = (k * 2 + p) * n_dp + v

    @pl.loop(1, count)
    def _(i):
        other = lax.rem(flat + i, count)
        pl.semaphore_signal(
            barrier,
            inc=1,
            device_id={
                "fsdp": other // (2 * n_dp),
                "pipe": lax.rem(other // n_dp, 2),
                "dp": lax.rem(other, n_dp),
            },
            device_id_type=MESH,
        )

    toks = mask_ref.shape[1]
    lane = lax.broadcasted_iota(jnp.int32, (1, toks), 1).astype(F32)
    fresh = mask_ref[...] > 0
    low = jnp.min(jnp.where(fresh, lane, float(toks)), axis=1, keepdims=True)
    high = jnp.max(jnp.where(fresh, lane, -1.0), axis=1, keepdims=True)
    hot_low = jnp.where(lane == low, 1.0, 0.0)
    hot_high = jnp.where(jnp.logical_and(lane == high, high > low), 1.0, 0.0)
    row8 = lax.broadcasted_iota(jnp.int32, (8, toks), 0)
    hot = jnp.where(row8 == 0, hot_low, jnp.where(row8 == 1, hot_high, 0.0))
    sel[...] = hot
    hot_b = hot.astype(BF16)
    live = jnp.sum(hot, axis=1, keepdims=True)[:FRESH]

    load_rows.wait()
    picked = dot_nn(hot_b, first[...])[:FRESH]

    @pl.when(is0)
    def _():
        xin[k] = picked.astype(BF16)

    pl.semaphore_wait(barrier, count - 1)

    def peer_copy(src, dst, send_sem, recv_sem, j, **where):
        return pltpu.make_async_remote_copy(
            src_ref=src,
            dst_ref=dst,
            send_sem=send_sem,
            recv_sem=recv_sem,
            device_id={"fsdp": j, "pipe": p, "dp": v, **where},
            device_id_type=MESH,
        )

    @pl.when(is0)
    def _():
        @pl.loop(1, n)
        def _(i):
            j = lax.rem(k + i, n)
            peer_copy(xin.at[k], xin.at[k], x_send.at[j], x_recv.at[k], j).start()

    sel_copy = peer_copy(sel, psel, sel_sems.at[0], sel_sems.at[1], k, pipe=1 - p)
    sel_copy.start()
    load_cached.wait()
    cached_rows = dot_nn(hot_b, cached[...])[:FRESH]
    sel_copy.wait()
    other_hot = psel[...]
    same_0 = jnp.sum(other_hot[:FRESH] * hot[0:1], axis=1, keepdims=True)
    same_1 = jnp.sum(other_hot[:FRESH] * hot[1:2], axis=1, keepdims=True)
    other_rows = dot_nn(other_hot.astype(BF16), cached[...])[:FRESH]
    step_val = jnp.full((1, rh), step_ref[0], jnp.int32)
    step_row = lax.broadcasted_iota(jnp.int32, bias_ref.shape, 0)
    bias_row = jnp.sum(jnp.where(step_row == step_ref[0], bias_ref[...], 0.0), axis=0, keepdims=True)
    load_up.wait()
    load_down.wait()

    @pl.when(is0)
    def _():
        @pl.loop(1, n)
        def _(i):
            j = lax.rem(k + i, n)
            peer_copy(xin.at[j], xin.at[j], x_send.at[j], x_recv.at[j], j).wait()

    @pl.when(is1)
    def _():
        @pl.loop(0, n)
        def _(j):
            peer_copy(xin.at[j], xin.at[j], x_send.at[j], x_recv.at[j], j, pipe=0).wait_recv()

    for j in range(n):
        x32[j * FRESH : (j + 1) * FRESH, :] = xin[j].astype(F32)
    scaled_all, _ = normalize(x32[...])
    x32[...] = scaled_all
    normed = scaled_all.astype(BF16)
    for j in range(n):

        @pl.when(k == j)
        def _():
            cols[v] = x32[:, j * cols_n : (j + 1) * cols_n].astype(BF16)

    router_part = dot_nn(cols[v], rin_ref[...])
    pre_act = dot_nt(normed, up[...])
    act, slope = gelu_both(pre_act)
    pre[...] = slope
    term = dot_nn(act.astype(BF16), down[...])
    for j in range(n):
        send1[j, :, :dim] = term[j * FRESH : (j + 1) * FRESH].astype(BF16)
        send1[j, :, dim:] = router_part[j * FRESH : (j + 1) * FRESH].astype(BF16)

    @pl.loop(1, n)
    def _(i):
        j = lax.rem(k + i, n)
        peer_copy(send1.at[j], recv1.at[k], r1_send.at[j], r1_recv.at[k], j).start()

    recv1[k] = send1[k]

    @pl.loop(1, n_dp)
    def _(i):
        u = lax.rem(v + i, n_dp)
        peer_copy(cols.at[v], cols.at[v], c_send.at[u], c_recv.at[v], k, dp=u).start()

    own_in = xin[k].astype(F32)
    own_scaled, own_inv = normalize(own_in)

    @pl.loop(1, n)
    def _(i):
        j = lax.rem(k + i, n)
        peer_copy(send1.at[j], recv1.at[j], r1_send.at[j], r1_recv.at[j], j).wait()

    summed = recv1[0].astype(F32)
    for j in range(1, n):
        summed = summed + recv1[j].astype(F32)
    fresh_out = own_in + summed[:, :dim]
    router_pre = summed[:, dim:] + bias_row
    router_act, router_slope = gelu_both(router_pre)
    r_out = rout_ref[...]
    gate = jax.nn.sigmoid(jnp.sum(router_act * r_out, axis=1, keepdims=True))
    gap = live * (fresh_out - cached_rows)
    new_rows = (cached_rows + gate * gap).astype(BF16).astype(F32)
    gate_slope = gate * (1.0 - gate)
    hid_factor = gate_slope * r_out * router_slope
    out_factor = gate_slope * router_act

    def blend_out():
        turned = jnp.transpose(hot)
        kept = cached[...].astype(F32)
        mixed = jnp.where(
            turned[:, 0:1] > 0.5,
            new_rows[0:1],
            jnp.where(turned[:, 1:2] > 0.5, new_rows[1:2], kept),
        )
        blend[...] = mixed.astype(BF16)
        pltpu.make_async_copy(blend, blended_hbm, out_sem).start()

    slot = v * n + k
    delta_copy = peer_copy(delta, delta_in, aux_sems.at[0], aux_sems.at[1], k, pipe=1 - p)
    factor_copy = peer_copy(factors, factors_in, aux_sems.at[2], aux_sems.at[3], k, pipe=1 - p)

    @pl.when(is0)
    def _():
        moved = jnp.where(
            same_0 > 0.5, new_rows[0:1], jnp.where(same_1 > 0.5, new_rows[1:2], other_rows)
        )
        in1[...] = moved.astype(BF16)

        @pl.loop(0, n)
        def _(i):
            j = lax.rem(k + i, n)
            peer_copy(in1, xin.at[k], f_send.at[j], x_recv.at[k], j, pipe=1).start()

        delta[...] = gap
        factors[0:FRESH, :] = hid_factor
        factors[FRESH : 2 * FRESH, :] = out_factor
        delta_copy.start()
        factor_copy.start()
        blend_out()

        @pl.loop(0, n)
        def _(j):
            peer_copy(in1, xin.at[j], f_send.at[j], x_recv.at[j], j, pipe=1).wait_send()

        delta_copy.wait_send()
        factor_copy.wait_send()

        @pl.loop(0, n * n_dp)
        def _(j):
            peer_copy(
                gmsg.at[j], gmsg.at[j], g_send.at[j], g_recv.at[j], k, pipe=1
            ).wait_recv()

    def message(ref, gate_grad, hid_fac, out_fac):
        ref[0:FRESH, :] = gate_grad * hid_fac
        ref[FRESH : FRESH + 1, :] = jnp.sum(gate_grad * out_fac, axis=0, keepdims=True)
        ref[FRESH + 1 : FRESH + 2, :] = step_val.astype(F32)

    @pl.when(is1)
    def _():
        gate_grad = jnp.sum(picked * gap, axis=1, keepdims=True)
        fresh_grad = picked * (live * gate)
        fgrad[k] = fresh_grad.astype(BF16)

        @pl.loop(1, n)
        def _(i):
            j = lax.rem(k + i, n)
            peer_copy(fgrad.at[k], fgrad.at[k], f_send.at[j], f_recv.at[k], j).start()

        message(gmsg.at[slot], gate_grad, hid_factor, out_factor)

        @pl.loop(1, n * n_dp)
        def _(i):
            t = lax.rem(slot + i, n * n_dp)
            peer_copy(
                gmsg.at[slot], gmsg.at[slot], g_send.at[t], g_recv.at[slot], lax.rem(t, n), dp=t // n
            ).start()

        blend_out()

        @pl.loop(1, n)
        def _(i):
            j = lax.rem(k + i, n)
            peer_copy(fgrad.at[j], fgrad.at[j], f_send.at[j], f_recv.at[j], j).wait()

        for j in range(n):
            x32[j * FRESH : (j + 1) * FRESH, :] = fgrad[j].astype(F32)
        act_grad = dot_nt(x32[...].astype(BF16), down[...])
        pre_grad = (act_grad * pre[...]).astype(BF16)
        total[...] = dot_nn(pre_grad, up[...])

        @pl.loop(1, n * n_dp)
        def _(i):
            t = lax.rem(slot + i, n * n_dp)
            peer_copy(
                gmsg.at[t], gmsg.at[t], g_send.at[t], g_recv.at[t], lax.rem(t, n), dp=t // n
            ).wait()

        for j in range(n):
            hid[j * FRESH : (j + 1) * FRESH, :] = gmsg[v * n + j, 0:FRESH, :]
        router_term = dot_nt(hid[0:rows, :].astype(BF16), rin_ref[...])
        for j in range(n):

            @pl.when(k == j)
            def _():
                total[:, j * cols_n : (j + 1) * cols_n] += router_term

        grads = total[...]
        for j in range(n):
            send2[j] = grads[j * FRESH : (j + 1) * FRESH].astype(BF16)

        @pl.loop(1, n)
        def _(i):
            j = lax.rem(k + i, n)
            peer_copy(send2.at[j], recv2.at[k], r2_send.at[j], r2_recv.at[k], j).start()

        recv2[k] = send2[k]
        delta_copy.wait_recv()
        factor_copy.wait_recv()

        @pl.loop(1, n)
        def _(i):
            j = lax.rem(k + i, n)
            peer_copy(send2.at[j], recv2.at[j], r2_send.at[j], r2_recv.at[j], j).wait()

        back = recv2[0].astype(F32)
        for j in range(1, n):
            back = back + recv2[j].astype(F32)
        input_grad = fresh_grad + normalize_back(own_scaled, own_inv, back)
        cot_first = same_0 * input_grad[0:1] + same_1 * input_grad[1:2]
        gate_grad_first = jnp.sum(cot_first * delta_in[...], axis=1, keepdims=True)
        message(
            gfirst,
            gate_grad_first,
            factors_in[0:FRESH, :],
            factors_in[FRESH : 2 * FRESH, :],
        )

        @pl.loop(0, n * n_dp)
        def _(i):
            t = lax.rem(slot + i, n * n_dp)
            peer_copy(
                gfirst, gmsg.at[slot], g_send.at[t], g_recv.at[slot], lax.rem(t, n), pipe=0, dp=t // n
            ).start()

    @pl.loop(1, n_dp)
    def _(i):
        u = lax.rem(v + i, n_dp)
        peer_copy(cols.at[u], cols.at[u], c_send.at[u], c_recv.at[u], k, dp=u).wait()

    bias_total = jnp.zeros(bias_grad_ref.shape, F32)
    out_total = jnp.zeros((1, rh), F32)
    step_all = step_row.astype(F32)
    for u in range(n_dp):
        summed_bias = jnp.zeros((1, rh), F32)
        for j in range(n):
            got = gmsg[u * n + j]
            hid[(u * n + j) * FRESH : (u * n + j + 1) * FRESH, :] = got[0:FRESH]
            summed_bias = summed_bias + jnp.sum(got[0:FRESH], axis=0, keepdims=True)
            out_total = out_total + got[FRESH : FRESH + 1]
        at = gmsg[u * n, FRESH + 1 : FRESH + 2, :]
        bias_total = bias_total + jnp.where(step_all == at, summed_bias, 0.0)
    bias_grad_ref[...] = bias_total
    out_grad_ref[...] = out_total
    cols_all = cols[...].reshape(n_dp * rows, cols_n)
    in_grad_ref[...] = dot_tn(cols_all, hid[...].astype(BF16))

    @pl.when(is1)
    def _():
        @pl.loop(0, n * n_dp)
        def _(t):
            peer_copy(
                gfirst, gmsg.at[t], g_send.at[t], g_recv.at[t], lax.rem(t, n), pipe=0, dp=t // n
            ).wait_send()

    pltpu.make_async_copy(blend, blended_hbm, out_sem).wait()


def body(
    n,
    n_dp,
    video_tokens,
    cached_out,
    fresh_mask,
    timestep,
    up_weight,
    down_weight,
    router_in,
    router_bias,
    router_out,
    out_cotangent,
):
    toks, dim = video_tokens.shape[1:]
    hidden = up_weight.shape[1]
    cols_n, rh = router_in.shape[1:]
    steps = router_bias.shape[1]
    rows = n * FRESH
    hbm = pl.BlockSpec(memory_space=pl.ANY)
    vmem = pl.BlockSpec(memory_space=pltpu.VMEM)
    smem = pl.BlockSpec(memory_space=pltpu.SMEM)
    dma = pltpu.SemaphoreType.DMA
    outs = pl.pallas_call(
        functools.partial(kernel, n, n_dp),
        out_shape=(
            jax.ShapeDtypeStruct((toks, dim), BF16),
            jax.ShapeDtypeStruct((cols_n, rh), F32),
            jax.ShapeDtypeStruct((steps, rh), F32),
            jax.ShapeDtypeStruct((1, rh), F32),
        ),
        in_specs=[hbm, hbm, vmem, smem, hbm, hbm, vmem, vmem, vmem, hbm],
        out_specs=(hbm, vmem, vmem, vmem),
        scratch_shapes=[
            pltpu.VMEM((hidden, dim), BF16),
            pltpu.VMEM((hidden, dim), BF16),
            pltpu.VMEM((toks, dim), BF16),
            pltpu.VMEM((toks, dim), BF16),
            pltpu.VMEM((toks, dim), BF16),
            pltpu.VMEM((8, toks), F32),
            pltpu.VMEM((8, toks), F32),
            pltpu.VMEM((n, FRESH, dim), BF16),
            pltpu.VMEM((FRESH, dim), BF16),
            pltpu.VMEM((rows, dim), F32),
            pltpu.VMEM((rows, hidden), F32),
            pltpu.VMEM((n, FRESH, dim + rh), BF16),
            pltpu.VMEM((n, FRESH, dim + rh), BF16),
            pltpu.VMEM((FRESH, dim), F32),
            pltpu.VMEM((FRESH, dim), F32),
            pltpu.VMEM((2 * FRESH, rh), F32),
            pltpu.VMEM((2 * FRESH, rh), F32),
            pltpu.VMEM((n, FRESH, dim), BF16),
            pltpu.VMEM((rows, dim), F32),
            pltpu.VMEM((n, FRESH, dim), BF16),
            pltpu.VMEM((n, FRESH, dim), BF16),
            pltpu.VMEM((n_dp, rows, cols_n), BF16),
            pltpu.VMEM((n * n_dp, FRESH + 2, rh), F32),
            pltpu.VMEM((FRESH + 2, rh), F32),
            pltpu.VMEM((n_dp * rows, rh), F32),
            dma((4,)),
            dma((2,)),
            dma((n,)),
            dma((n,)),
            dma((n,)),
            dma((n,)),
            dma((4,)),
            dma((n,)),
            dma((n,)),
            dma((n,)),
            dma((n,)),
            dma((n_dp,)),
            dma((n_dp,)),
            dma((n * n_dp,)),
            dma((n * n_dp,)),
            dma,
        ],
        compiler_params=pltpu.CompilerParams(
            collective_id=0, has_side_effects=True, vmem_limit_bytes=48 * 1024 * 1024
        ),
    )(
        video_tokens[0],
        cached_out[0, 0],
        fresh_mask[0],
        timestep,
        up_weight[0],
        down_weight[0],
        router_in[0],
        router_bias[0],
        router_out,
        out_cotangent[0],
    )
    blended, in_grad, bias_grad, out_grad = outs
    return (blended[None, None], in_grad[None], bias_grad[None], out_grad)


def solution(mesh):
    placed = (
        P("dp", "fsdp", None),
        P("pipe", "dp", "fsdp", None),
        P("pipe", "dp", "fsdp"),
        P("dp"),
        P("pipe", "fsdp", None),
        P("pipe", "fsdp", None),
        P("pipe", "fsdp", None),
        P("pipe", None, None),
        P("pipe", None),
        P("dp", "fsdp", None),
    )
    return jax.shard_map(
        functools.partial(body, mesh.shape["fsdp"], mesh.shape["dp"]),
        mesh=mesh,
        in_specs=placed,
        out_specs=(
            P("pipe", "dp", "fsdp", None),
            P("pipe", "fsdp", None),
            P("pipe", None, None),
            P("pipe", None),
        ),
        check_vma=False,
    )
```

time: 422 us -> 53.8 us (0.13)
  blocking collectives: 185 us -> 0 us
  waiting for transfers between devices: 168 us -> 0 us
  Pallas kernels: 0 us -> 43 us
  matrix products: 22.2 us -> 0 us
  other arithmetic: 20.6 us -> 0 us
  between operations: 16 us -> 1.29 us
    unnamed x7 -> x0, waiting for transfers between devices: 158 us -> none
    all_gather x3 -> x0, blocking collectives: 93.5 us -> none  [the longest x2 62.9 us: forward(): gathered = lax.all_gather(normed, 'fsdp', axis=0, tiled=True)]
    psum x3 -> x0, blocking collectives: 51 us -> none  [the longest x2 42.1 us: forward(): lax.psum(router_part.astype(jnp.bfloat16), 'fsdp').astype(jnp.float32)]
    pallas_call x0 -> x1, Pallas kernels: none -> 43 us  [body(): pl.pallas_call(functools.partial(kernel, n, n_dp), out_shape=(jax.ShapeDt...]
    unnamed x2 -> x0, blocking collectives: 40.3 us -> none
    dot_general x14 -> x0, matrix products: 22.2 us -> none  [the longest x2 10.2 us: forward(): jnp.dot(hid_act, w_down, preferred_element_type=jnp.float32)]
    psum x1 -> x0, waiting for transfers between devices: 9.1 us -> none  [body(): lax.psum(for_sending(chosen), 'dp')]
    unnamed x21 -> x17, local copies, waits for them, and re-layouts: 1.3 us -> 9.11 us
  transfers between devices with their start and end apart: 7 -> 0, of which waited for: 5 -> 0; matrix products, arithmetic and copies ran while one was open for 2% -> 0% of each run, Pallas kernels for 0% -> 0%
where the time goes in v1:
time: 53.8 us; the launch traced here: 53.4 us
  Pallas kernels  43 us (80%)
  local copies, waits for them, and re-layouts  9.11 us (17%)
  between operations  1.29 us (2%)
    pallas_call x1, Pallas kernels, body(): pl.pallas_call(functools.partial(kernel, n, n_dp), out_shape=(jax.ShapeDt...  43 us
    unnamed x17, local copies, waits for them, and re-layouts  9.11 us

profile of v1, /device:TPU:0, one launch (start us, length us, event | category | flops | bytes accessed | tf_op | source)
XLA Modules:
  0.0 53.4 jit_solution(17608890108505756592)
XLA Ops:
  1.3 0.8 %copy.17 = f32[1,50,256]{2,1,0:T(8,128)S(1)} copy(f32[1,50,256]{2,0,1:T(1,128)} %param.17) | data formatting | bytes 102400
  2.1 0.0 copy-start
  2.1 1.1 %copy-done = bf16[1,128,2560]{2,1,0:T(8,128)(2,1)S(1)} copy-done((bf16[1,128,2560]{2,1,0:T(8,128)(2,1)S(1)}, bf16[1,128,2560]{2,1,0:T(8,128)(2,1)}, u32[]{:S(2)}) %copy-start) | copy-done | bytes 655384
  3.2 0.0 copy-start.1
  3.2 1.1 %copy-done.1 = bf16[1,1,128,2560]{3,2,1,0:T(8,128)(2,1)S(1)} copy-done((bf16[1,1,128,2560]{3,2,1,0:T(8,128)(2,1)S(1)}, bf16[1,1,128,2560]{3,2,1,0:T(8,128)(2,1)}, u32[]{:S(2)}) %copy-start.1) | copy-done | bytes 655384
  4.3 0.0 copy-start.2
  4.3 1.1 %copy-done.2 = bf16[1,128,2560]{2,1,0:T(8,128)(2,1)S(1)} copy-done((bf16[1,128,2560]{2,1,0:T(8,128)(2,1)S(1)}, bf16[1,128,2560]{2,1,0:T(8,128)(2,1)}, u32[]{:S(2)}) %copy-start.2) | copy-done | bytes 655384
  5.4 0.0 copy-start.3
  5.4 0.9 %copy-done.3 = bf16[1,320,256]{2,1,0:T(8,128)(2,1)S(1)} copy-done((bf16[1,320,256]{2,1,0:T(8,128)(2,1)S(1)}, bf16[1,320,256]{2,1,0:T(8,128)(2,1)}, u32[]{:S(2)}) %copy-start.3) | copy-done | bytes 163864
  6.3 0.0 copy-start.4
  6.3 0.7 %copy-done.4 = f32[1,256]{1,0:T(1,128)S(1)} copy-done((f32[1,256]{1,0:T(1,128)S(1)}, f32[1,256]{1,0:T(1,128)}, u32[]{:S(2)}) %copy-start.4) | copy-done | bytes 1048
  6.9 0.0 copy-start.5
  6.9 0.7 %copy-done.5 = s32[1,1,128]{2,1,0:T(1,128)S(1)} copy-done((s32[1,1,128]{2,1,0:T(1,128)S(1)}, s32[1,1,128]{2,1,0:T(1,128)}, u32[]{:S(2)}) %copy-start.5) | copy-done | bytes 536
  7.6 43.0 %shard_map.129 = (bf16[128,2560]{1,0:T(8,128)(2,1)S(1)}, f32[320,256]{1,0:T(8,128)S(1)}, f32[50,256]{1,0:T(8,128)S(1)}, f32[1,256]{1,0:T(1,128)S(1)}) custom-call(bf16[128,2560]{1,0:T(8,128)(2,1)S(1)} %bitcast.14, bf16[128,2560]{1,0:T(8,128)(2,1)S(1)} %bitcast.15, s32[1,128]{1,0:T(1,128)S(1)} %bitcast.21, s32[1]{0:T(128)S(6)} %copy.21.step_ref, ...), custom_call_target="tpu_custom_call" | custom-call | tf_op jit(solution)/shard_map/pallas_call | solution.py:477
  50.6 0.7 %copy.14 = f32[1,50,256]{2,0,1:T(1,128)} copy(f32[1,50,256]{2,1,0:T(8,128)S(1)} %bitcast.20) | data formatting | bytes 102400
  51.3 0.8 %copy.22 = bf16[1,1,128,2560]{3,2,1,0:T(8,128)(2,1)} copy(bf16[1,1,128,2560]{3,2,1,0:T(8,128)(2,1)S(1)} %bitcast.13) | data formatting | bytes 1310720
  52.2 0.7 %copy.23 = f32[1,320,256]{2,1,0:T(8,128)} copy(f32[1,320,256]{2,1,0:T(8,128)S(1)} %bitcast.17) | data formatting | bytes 655360
  52.9 0.6 %copy.24 = f32[1,256]{1,0:T(1,128)} copy(f32[1,256]{1,0:T(1,128)S(1)} %get-tuple-element.23) | data formatting | bytes 2048
Async XLA Ops:
  2.1 1.1 %copy-start = (bf16[1,128,2560]{2,1,0:T(8,128)(2,1)S(1)}, bf16[1,128,2560]{2,1,0:T(8,128)(2,1)}, u32[]{:S(2)}) copy-start(bf16[1,128,2560]{2,1,0:T(8,128)(2,1)} %param.10) | copy-start | bytes 1966084
  3.2 1.1 %copy-start.1 = (bf16[1,1,128,2560]{3,2,1,0:T(8,128)(2,1)S(1)}, bf16[1,1,128,2560]{3,2,1,0:T(8,128)(2,1)}, u32[]{:S(2)}) copy-start(bf16[1,1,128,2560]{3,2,1,0:T(8,128)(2,1)} %param.11) | copy-start | bytes 1966084
  4.3 1.1 %copy-start.2 = (bf16[1,128,2560]{2,1,0:T(8,128)(2,1)S(1)}, bf16[1,128,2560]{2,1,0:T(8,128)(2,1)}, u32[]{:S(2)}) copy-start(bf16[1,128,2560]{2,1,0:T(8,128)(2,1)} %param.19) | copy-start | bytes 1966084
  5.4 0.9 %copy-start.3 = (bf16[1,320,256]{2,1,0:T(8,128)(2,1)S(1)}, bf16[1,320,256]{2,1,0:T(8,128)(2,1)}, u32[]{:S(2)}) copy-start(bf16[1,320,256]{2,1,0:T(8,128)(2,1)} %param.16) | copy-start | bytes 491524
  6.3 0.7 %copy-start.4 = (f32[1,256]{1,0:T(1,128)S(1)}, f32[1,256]{1,0:T(1,128)}, u32[]{:S(2)}) copy-start(f32[1,256]{1,0:T(1,128)} %rout_ref.1) | copy-start | bytes 3076
  6.9 0.7 %copy-start.5 = (s32[1,1,128]{2,1,0:T(1,128)S(1)}, s32[1,1,128]{2,1,0:T(1,128)}, u32[]{:S(2)}) copy-start(s32[1,1,128]{2,1,0:T(1,128)} %param.12) | copy-start | bytes 1540

commit v2 on v1

--- a/solution.py
+++ b/solution.py
@@ -58,39 +58,50 @@
     n_dp,
     tokens_hbm,
     cached_hbm,
-    mask_ref,
+    mask_hbm,
     step_ref,
     up_hbm,
     down_hbm,
-    rin_ref,
-    bias_ref,
-    rout_ref,
+    rin_hbm,
+    bias_hbm,
+    rout_hbm,
     cot_hbm,
     blended_hbm,
-    in_grad_ref,
-    bias_grad_ref,
-    out_grad_ref,
+    in_grad_hbm,
+    bias_grad_hbm,
+    out_grad_hbm,
     up,
     down,
     first,
     cached,
     blend,
+    mask_ref,
+    rin_ref,
+    bias_ref,
+    rout_ref,
+    in_grad_ref,
+    bias_grad_ref,
+    out_grad_ref,
     sel,
     psel,
     xin,
+    win,
+    cin,
     in1,
+    w1,
     x32,
-    pre,
+    c32,
+    part_s,
+    slope_ref,
+    act_grad,
     send1,
     recv1,
+    send2,
+    recv2,
     delta,
     delta_in,
     factors,
     factors_in,
-    fgrad,
-    total,
-    send2,
-    recv2,
     cols,
     gmsg,
     gfirst,
@@ -99,13 +110,14 @@
     sel_sems,
     x_send,
     x_recv,
+    w_send,
+    w_recv,
     r1_send,
     r1_recv,
+    r2_send,
+    r2_recv,
     aux_sems,
     f_send,
-    f_recv,
-    r2_send,
-    r2_recv,
     c_send,
     c_recv,
     g_send,
@@ -122,11 +134,18 @@
     cols_n = rin_ref.shape[0]
     rows = n * FRESH
 
-    load_rows = pltpu.make_async_copy(tokens_hbm, first, load_sem.at[0])
-    load_cot = pltpu.make_async_copy(cot_hbm, first, load_sem.at[0])
-    load_cached = pltpu.make_async_copy(cached_hbm, cached, load_sem.at[1])
-    load_up = pltpu.make_async_copy(up_hbm, up, load_sem.at[2])
-    load_down = pltpu.make_async_copy(down_hbm, down, load_sem.at[3])
+    load_mask = pltpu.make_async_copy(mask_hbm, mask_ref, load_sem.at[0])
+    load_rows = pltpu.make_async_copy(tokens_hbm, first, load_sem.at[1])
+    load_cot = pltpu.make_async_copy(cot_hbm, first, load_sem.at[1])
+    later = [
+        pltpu.make_async_copy(cached_hbm, cached, load_sem.at[2]),
+        pltpu.make_async_copy(up_hbm, up, load_sem.at[3]),
+        pltpu.make_async_copy(down_hbm, down, load_sem.at[4]),
+        pltpu.make_async_copy(rin_hbm, rin_ref, load_sem.at[5]),
+        pltpu.make_async_copy(bias_hbm, bias_ref, load_sem.at[6]),
+        pltpu.make_async_copy(rout_hbm, rout_ref, load_sem.at[7]),
+    ]
+    load_mask.start()
 
     @pl.when(is0)
     def _():
@@ -135,10 +154,6 @@
     @pl.when(is1)
     def _():
         load_cot.start()
-
-    load_cached.start()
-    load_up.start()
-    load_down.start()
 
     barrier = pltpu.get_barrier_semaphore()
     count = n * 2 * n_dp
@@ -158,6 +173,10 @@
             device_id_type=MESH,
         )
 
+    for load in later:
+        load.start()
+
+    load_mask.wait()
     toks = mask_ref.shape[1]
     lane = lax.broadcasted_iota(jnp.int32, (1, toks), 1).astype(F32)
     fresh = mask_ref[...] > 0
@@ -178,6 +197,10 @@
     def _():
         xin[k] = picked.astype(BF16)
 
+    @pl.when(is1)
+    def _():
+        cin[k] = picked.astype(BF16)
+
     pl.semaphore_wait(barrier, count - 1)
 
     def peer_copy(src, dst, send_sem, recv_sem, j, **where):
@@ -197,9 +220,17 @@
             j = lax.rem(k + i, n)
             peer_copy(xin.at[k], xin.at[k], x_send.at[j], x_recv.at[k], j).start()
 
+    @pl.when(is1)
+    def _():
+        @pl.loop(1, n)
+        def _(i):
+            j = lax.rem(k + i, n)
+            peer_copy(cin.at[k], cin.at[k], x_send.at[j], c_recv.at[k], j).start()
+
     sel_copy = peer_copy(sel, psel, sel_sems.at[0], sel_sems.at[1], k, pipe=1 - p)
     sel_copy.start()
-    load_cached.wait()
+    for load in later:
+        load.wait()
     cached_rows = dot_nn(hot_b, cached[...])[:FRESH]
     sel_copy.wait()
     other_hot = psel[...]
@@ -207,10 +238,8 @@
     same_1 = jnp.sum(other_hot[:FRESH] * hot[1:2], axis=1, keepdims=True)
     other_rows = dot_nn(other_hot.astype(BF16), cached[...])[:FRESH]
     step_val = jnp.full((1, rh), step_ref[0], jnp.int32)
-    step_row = lax.broadcasted_iota(jnp.int32, bias_ref.shape, 0)
-    bias_row = jnp.sum(jnp.where(step_row == step_ref[0], bias_ref[...], 0.0), axis=0, keepdims=True)
-    load_up.wait()
-    load_down.wait()
+    bias_row = bias_ref[step_ref[0]]
+    r_out = rout_ref[...]
 
     @pl.when(is0)
     def _():
@@ -221,6 +250,15 @@
 
     @pl.when(is1)
     def _():
+        @pl.loop(1, n)
+        def _(i):
+            j = lax.rem(k + i, n)
+            peer_copy(cin.at[j], cin.at[j], x_send.at[j], c_recv.at[j], j).wait()
+
+        for j in range(n):
+            c32[j * FRESH : (j + 1) * FRESH, :] = cin[j].astype(F32)
+        act_grad[...] = dot_nt(c32[...].astype(BF16), down[...])
+
         @pl.loop(0, n)
         def _(j):
             peer_copy(xin.at[j], xin.at[j], x_send.at[j], x_recv.at[j], j, pipe=0).wait_recv()
@@ -239,7 +277,7 @@
     router_part = dot_nn(cols[v], rin_ref[...])
     pre_act = dot_nt(normed, up[...])
     act, slope = gelu_both(pre_act)
-    pre[...] = slope
+    slope_ref[...] = slope
     term = dot_nn(act.astype(BF16), down[...])
     for j in range(n):
         send1[j, :, :dim] = term[j * FRESH : (j + 1) * FRESH].astype(BF16)
@@ -250,15 +288,43 @@
         j = lax.rem(k + i, n)
         peer_copy(send1.at[j], recv1.at[k], r1_send.at[j], r1_recv.at[k], j).start()
 
+    @pl.when(is1)
+    def _():
+        @pl.loop(0, n)
+        def _(j):
+            peer_copy(win.at[j], win.at[j], x_send.at[j], w_recv.at[j], j, pipe=0).wait_recv()
+
+        for j in range(n):
+            c32[j * FRESH : (j + 1) * FRESH, :] = win[j].astype(F32)
+        for j in range(n):
+
+            @pl.when(k == j)
+            def _():
+                part_s[:, 0:rh] = dot_nn(
+                    c32[:, j * cols_n : (j + 1) * cols_n].astype(BF16), rin_ref[...]
+                )
+
+        up_w = dot_nt(c32[...].astype(BF16), up[...])
+        along = jnp.sum(act_grad[...] * slope_ref[...] * up_w, axis=1, keepdims=True)
+        part_s[:, rh:] = jnp.broadcast_to(along, (rows, part_s.shape[1] - rh))
+        for j in range(n):
+            send2[j] = part_s[j * FRESH : (j + 1) * FRESH, :]
+
+        @pl.loop(1, n)
+        def _(i):
+            j = lax.rem(k + i, n)
+            peer_copy(send2.at[j], recv2.at[k], r2_send.at[j], r2_recv.at[k], j).start()
+
+        recv2[k] = send2[k]
+
     recv1[k] = send1[k]
 
     @pl.loop(1, n_dp)
     def _(i):
         u = lax.rem(v + i, n_dp)
-        peer_copy(cols.at[v], cols.at[v], c_send.at[u], c_recv.at[v], k, dp=u).start()
+        peer_copy(cols.at[v], cols.at[v], c_send.at[u], g_recv.at[n * n_dp + v], k, dp=u).start()
 
     own_in = xin[k].astype(F32)
-    own_scaled, own_inv = normalize(own_in)
 
     @pl.loop(1, n)
     def _(i):
@@ -271,7 +337,6 @@
     fresh_out = own_in + summed[:, :dim]
     router_pre = summed[:, dim:] + bias_row
     router_act, router_slope = gelu_both(router_pre)
-    r_out = rout_ref[...]
     gate = jax.nn.sigmoid(jnp.sum(router_act * r_out, axis=1, keepdims=True))
     gap = live * (fresh_out - cached_rows)
     new_rows = (cached_rows + gate * gap).astype(BF16).astype(F32)
@@ -288,7 +353,7 @@
             jnp.where(turned[:, 1:2] > 0.5, new_rows[1:2], kept),
         )
         blend[...] = mixed.astype(BF16)
-        pltpu.make_async_copy(blend, blended_hbm, out_sem).start()
+        pltpu.make_async_copy(blend, blended_hbm, out_sem.at[0]).start()
 
     slot = v * n + k
     delta_copy = peer_copy(delta, delta_in, aux_sems.at[0], aux_sems.at[1], k, pipe=1 - p)
@@ -306,7 +371,16 @@
             j = lax.rem(k + i, n)
             peer_copy(in1, xin.at[k], f_send.at[j], x_recv.at[k], j, pipe=1).start()
 
-        delta[...] = gap
+        met = same_0 * gap[0:1] + same_1 * gap[1:2]
+        scaled, inv_std = normalize(moved)
+        w1[...] = normalize_back(scaled, inv_std, met).astype(BF16)
+
+        @pl.loop(0, n)
+        def _(i):
+            j = lax.rem(k + i, n)
+            peer_copy(w1, win.at[k], w_send.at[j], w_recv.at[k], j, pipe=1).start()
+
+        delta[...] = met
         factors[0:FRESH, :] = hid_factor
         factors[FRESH : 2 * FRESH, :] = out_factor
         delta_copy.start()
@@ -316,6 +390,7 @@
         @pl.loop(0, n)
         def _(j):
             peer_copy(in1, xin.at[j], f_send.at[j], x_recv.at[j], j, pipe=1).wait_send()
+            peer_copy(w1, win.at[j], w_send.at[j], w_recv.at[j], j, pipe=1).wait_send()
 
         delta_copy.wait_send()
         factor_copy.wait_send()
@@ -334,14 +409,6 @@
     @pl.when(is1)
     def _():
         gate_grad = jnp.sum(picked * gap, axis=1, keepdims=True)
-        fresh_grad = picked * (live * gate)
-        fgrad[k] = fresh_grad.astype(BF16)
-
-        @pl.loop(1, n)
-        def _(i):
-            j = lax.rem(k + i, n)
-            peer_copy(fgrad.at[k], fgrad.at[k], f_send.at[j], f_recv.at[k], j).start()
-
         message(gmsg.at[slot], gate_grad, hid_factor, out_factor)
 
         @pl.loop(1, n * n_dp)
@@ -351,59 +418,22 @@
                 gmsg.at[slot], gmsg.at[slot], g_send.at[t], g_recv.at[slot], lax.rem(t, n), dp=t // n
             ).start()
 
-        blend_out()
-
-        @pl.loop(1, n)
-        def _(i):
-            j = lax.rem(k + i, n)
-            peer_copy(fgrad.at[j], fgrad.at[j], f_send.at[j], f_recv.at[j], j).wait()
-
-        for j in range(n):
-            x32[j * FRESH : (j + 1) * FRESH, :] = fgrad[j].astype(F32)
-        act_grad = dot_nt(x32[...].astype(BF16), down[...])
-        pre_grad = (act_grad * pre[...]).astype(BF16)
-        total[...] = dot_nn(pre_grad, up[...])
-
-        @pl.loop(1, n * n_dp)
-        def _(i):
-            t = lax.rem(slot + i, n * n_dp)
-            peer_copy(
-                gmsg.at[t], gmsg.at[t], g_send.at[t], g_recv.at[t], lax.rem(t, n), dp=t // n
-            ).wait()
-
-        for j in range(n):
-            hid[j * FRESH : (j + 1) * FRESH, :] = gmsg[v * n + j, 0:FRESH, :]
-        router_term = dot_nt(hid[0:rows, :].astype(BF16), rin_ref[...])
-        for j in range(n):
-
-            @pl.when(k == j)
-            def _():
-                total[:, j * cols_n : (j + 1) * cols_n] += router_term
-
-        grads = total[...]
-        for j in range(n):
-            send2[j] = grads[j * FRESH : (j + 1) * FRESH].astype(BF16)
-
-        @pl.loop(1, n)
-        def _(i):
-            j = lax.rem(k + i, n)
-            peer_copy(send2.at[j], recv2.at[k], r2_send.at[j], r2_recv.at[k], j).start()
-
-        recv2[k] = send2[k]
         delta_copy.wait_recv()
         factor_copy.wait_recv()
+        straight = jnp.sum(picked * delta_in[...], axis=1, keepdims=True)
 
         @pl.loop(1, n)
         def _(i):
             j = lax.rem(k + i, n)
             peer_copy(send2.at[j], recv2.at[j], r2_send.at[j], r2_recv.at[j], j).wait()
 
-        back = recv2[0].astype(F32)
+        through = recv2[0]
         for j in range(1, n):
-            back = back + recv2[j].astype(F32)
-        input_grad = fresh_grad + normalize_back(own_scaled, own_inv, back)
-        cot_first = same_0 * input_grad[0:1] + same_1 * input_grad[1:2]
-        gate_grad_first = jnp.sum(cot_first * delta_in[...], axis=1, keepdims=True)
+            through = through + recv2[j]
+        met_grad = live * gate * (straight + through[:, rh : rh + 1]) + jnp.sum(
+            gate_grad * hid_factor * through[:, 0:rh], axis=1, keepdims=True
+        )
+        gate_grad_first = same_0 * met_grad[0:1] + same_1 * met_grad[1:2]
         message(
             gfirst,
             gate_grad_first,
@@ -415,17 +445,31 @@
         def _(i):
             t = lax.rem(slot + i, n * n_dp)
             peer_copy(
-                gfirst, gmsg.at[slot], g_send.at[t], g_recv.at[slot], lax.rem(t, n), pipe=0, dp=t // n
+                gfirst,
+                gmsg.at[slot],
+                g_send.at[n * n_dp + t],
+                g_recv.at[slot],
+                lax.rem(t, n),
+                pipe=0,
+                dp=t // n,
             ).start()
+
+        blend_out()
+
+        @pl.loop(1, n * n_dp)
+        def _(i):
+            t = lax.rem(slot + i, n * n_dp)
+            peer_copy(
+                gmsg.at[t], gmsg.at[t], g_send.at[t], g_recv.at[t], lax.rem(t, n), dp=t // n
+            ).wait()
 
     @pl.loop(1, n_dp)
     def _(i):
         u = lax.rem(v + i, n_dp)
-        peer_copy(cols.at[u], cols.at[u], c_send.at[u], c_recv.at[u], k, dp=u).wait()
-
-    bias_total = jnp.zeros(bias_grad_ref.shape, F32)
+        peer_copy(cols.at[u], cols.at[u], c_send.at[u], g_recv.at[n * n_dp + u], k, dp=u).wait()
+
     out_total = jnp.zeros((1, rh), F32)
-    step_all = step_row.astype(F32)
+    bias_sums = []
     for u in range(n_dp):
         summed_bias = jnp.zeros((1, rh), F32)
         for j in range(n):
@@ -433,22 +477,40 @@
             hid[(u * n + j) * FRESH : (u * n + j + 1) * FRESH, :] = got[0:FRESH]
             summed_bias = summed_bias + jnp.sum(got[0:FRESH], axis=0, keepdims=True)
             out_total = out_total + got[FRESH : FRESH + 1]
-        at = gmsg[u * n, FRESH + 1 : FRESH + 2, :]
-        bias_total = bias_total + jnp.where(step_all == at, summed_bias, 0.0)
+        bias_sums.append((gmsg[u * n, FRESH + 1 : FRESH + 2, :], summed_bias))
+    cols_all = cols[...].reshape(n_dp * rows, cols_n)
+    in_grad_ref[...] = dot_tn(cols_all, hid[...].astype(BF16))
+    put_in = pltpu.make_async_copy(in_grad_ref, in_grad_hbm, out_sem.at[1])
+    put_in.start()
+    step_all = lax.broadcasted_iota(jnp.int32, bias_grad_ref.shape, 0).astype(F32)
+    bias_total = jnp.zeros(bias_grad_ref.shape, F32)
+    for at, summed_bias in bias_sums:
+        bias_total = bias_total + jnp.where(step_all == at[None], summed_bias[None], 0.0)
     bias_grad_ref[...] = bias_total
     out_grad_ref[...] = out_total
-    cols_all = cols[...].reshape(n_dp * rows, cols_n)
-    in_grad_ref[...] = dot_tn(cols_all, hid[...].astype(BF16))
+    put_bias = pltpu.make_async_copy(bias_grad_ref, bias_grad_hbm, out_sem.at[2])
+    put_out = pltpu.make_async_copy(out_grad_ref, out_grad_hbm, out_sem.at[3])
+    put_bias.start()
+    put_out.start()
 
     @pl.when(is1)
     def _():
         @pl.loop(0, n * n_dp)
         def _(t):
             peer_copy(
-                gfirst, gmsg.at[t], g_send.at[t], g_recv.at[t], lax.rem(t, n), pipe=0, dp=t // n
+                gfirst,
+                gmsg.at[t],
+                g_send.at[n * n_dp + t],
+                g_recv.at[t],
+                lax.rem(t, n),
+                pipe=0,
+                dp=t // n,
             ).wait_send()
 
-    pltpu.make_async_copy(blend, blended_hbm, out_sem).wait()
+    pltpu.make_async_copy(blend, blended_hbm, out_sem.at[0]).wait()
+    put_in.wait()
+    put_bias.wait()
+    put_out.wait()
 
 
 def body(
@@ -471,7 +533,6 @@
     steps = router_bias.shape[1]
     rows = n * FRESH
     hbm = pl.BlockSpec(memory_space=pl.ANY)
-    vmem = pl.BlockSpec(memory_space=pltpu.VMEM)
     smem = pl.BlockSpec(memory_space=pltpu.SMEM)
     dma = pltpu.SemaphoreType.DMA
     outs = pl.pallas_call(
@@ -479,56 +540,68 @@
         out_shape=(
             jax.ShapeDtypeStruct((toks, dim), BF16),
             jax.ShapeDtypeStruct((cols_n, rh), F32),
-            jax.ShapeDtypeStruct((steps, rh), F32),
+            jax.ShapeDtypeStruct((steps, 1, rh), F32),
             jax.ShapeDtypeStruct((1, rh), F32),
         ),
-        in_specs=[hbm, hbm, vmem, smem, hbm, hbm, vmem, vmem, vmem, hbm],
-        out_specs=(hbm, vmem, vmem, vmem),
+        in_specs=[hbm, hbm, hbm, smem] + [hbm] * 6,
+        out_specs=(hbm,) * 4,
         scratch_shapes=[
             pltpu.VMEM((hidden, dim), BF16),
             pltpu.VMEM((hidden, dim), BF16),
             pltpu.VMEM((toks, dim), BF16),
             pltpu.VMEM((toks, dim), BF16),
             pltpu.VMEM((toks, dim), BF16),
+            pltpu.VMEM((1, toks), jnp.int32),
+            pltpu.VMEM((cols_n, rh), BF16),
+            pltpu.VMEM((steps, 1, rh), F32),
+            pltpu.VMEM((1, rh), F32),
+            pltpu.VMEM((cols_n, rh), F32),
+            pltpu.VMEM((steps, 1, rh), F32),
+            pltpu.VMEM((1, rh), F32),
             pltpu.VMEM((8, toks), F32),
             pltpu.VMEM((8, toks), F32),
             pltpu.VMEM((n, FRESH, dim), BF16),
+            pltpu.VMEM((n, FRESH, dim), BF16),
+            pltpu.VMEM((n, FRESH, dim), BF16),
+            pltpu.VMEM((FRESH, dim), BF16),
             pltpu.VMEM((FRESH, dim), BF16),
             pltpu.VMEM((rows, dim), F32),
+            pltpu.VMEM((rows, dim), F32),
+            pltpu.VMEM((rows, rh + 128), F32),
+            pltpu.VMEM((rows, hidden), F32),
             pltpu.VMEM((rows, hidden), F32),
             pltpu.VMEM((n, FRESH, dim + rh), BF16),
             pltpu.VMEM((n, FRESH, dim + rh), BF16),
+            pltpu.VMEM((n, FRESH, rh + 128), F32),
+            pltpu.VMEM((n, FRESH, rh + 128), F32),
             pltpu.VMEM((FRESH, dim), F32),
             pltpu.VMEM((FRESH, dim), F32),
             pltpu.VMEM((2 * FRESH, rh), F32),
             pltpu.VMEM((2 * FRESH, rh), F32),
-            pltpu.VMEM((n, FRESH, dim), BF16),
-            pltpu.VMEM((rows, dim), F32),
-            pltpu.VMEM((n, FRESH, dim), BF16),
-            pltpu.VMEM((n, FRESH, dim), BF16),
             pltpu.VMEM((n_dp, rows, cols_n), BF16),
             pltpu.VMEM((n * n_dp, FRESH + 2, rh), F32),
             pltpu.VMEM((FRESH + 2, rh), F32),
             pltpu.VMEM((n_dp * rows, rh), F32),
+            dma((8,)),
+            dma((2,)),
+            dma((n,)),
+            dma((n,)),
+            dma((n,)),
+            dma((n,)),
+            dma((n,)),
+            dma((n,)),
+            dma((n,)),
+            dma((n,)),
             dma((4,)),
-            dma((2,)),
-            dma((n,)),
-            dma((n,)),
-            dma((n,)),
-            dma((n,)),
+            dma((n,)),
+            dma((n_dp,)),
+            dma((n,)),
+            dma((2 * n * n_dp,)),
+            dma((n * n_dp + n_dp,)),
             dma((4,)),
-            dma((n,)),
-            dma((n,)),
-            dma((n,)),
-            dma((n,)),
-            dma((n_dp,)),
-            dma((n_dp,)),
-            dma((n * n_dp,)),
-            dma((n * n_dp,)),
-            dma,
         ],
         compiler_params=pltpu.CompilerParams(
-            collective_id=0, has_side_effects=True, vmem_limit_bytes=48 * 1024 * 1024
+            collective_id=0, has_side_effects=True, vmem_limit_bytes=67043328
         ),
     )(
         video_tokens[0],
@@ -538,12 +611,12 @@
         up_weight[0],
         down_weight[0],
         router_in[0],
-        router_bias[0],
+        jnp.transpose(router_bias, (1, 0, 2)),
         router_out,
         out_cotangent[0],
     )
     blended, in_grad, bias_grad, out_grad = outs
-    return (blended[None, None], in_grad[None], bias_grad[None], out_grad)
+    return (blended[None, None], in_grad[None], jnp.transpose(bias_grad, (1, 0, 2)), out_grad)
 
 
 def solution(mesh):

time: 53.8 us -> 43.5 us (0.81)
  Pallas kernels: 43 us -> 35.6 us
  local copies, waits for them, and re-layouts: 9.11 us -> 6.35 us
    pallas_call x1, Pallas kernels: 43 us -> 35.6 us  [body(): pl.pallas_call(functools.partial(kernel, n, n_dp), out_shape=(jax.ShapeDt...]
    unnamed x17 -> x4, local copies, waits for them, and re-layouts: 9.11 us -> 6.35 us
where the time goes in v2:
time: 43.5 us; the launch traced here: 43.2 us
  Pallas kernels  35.6 us (82%)
  local copies, waits for them, and re-layouts  6.35 us (15%)
  between operations  1.29 us (3%)
    pallas_call x1, Pallas kernels, body(): pl.pallas_call(functools.partial(kernel, n, n_dp), out_shape=(jax.ShapeDt...  35.6 us
    unnamed x4, local copies, waits for them, and re-layouts  6.35 us

profile of v2, /device:TPU:0, one launch (start us, length us, event | category | flops | bytes accessed | tf_op | source)
XLA Modules:
  0.0 43.2 jit_solution(15561650883772231015)
XLA Ops:
  1.3 35.6 %shard_map.129 = (bf16[128,2560]{1,0:T(8,128)(2,1)}, f32[320,256]{1,0:T(8,128)}, f32[50,1,256]{2,1,0:T(1,128)}, f32[1,256]{1,0:T(1,128)}) custom-call(bf16[128,2560]{1,0:T(8,128)(2,1)} %bitcast.14, bf16[128,2560]{1,0:T(8,128)(2,1)} %bitcast.15, s32[1,128]{1,0:T(1,128)} %bitcast.21, s32[1]{0:T(128)S(6)} %copy.18.step_ref, bf16[896,2560]{1,0:T(8,128)(2,1)} %bitcast.11, ...), custom_call_target="tpu_custom_call" | custom-call | tf_op jit(solution)/shard_map/pallas_call | solution.py:538
  36.9 2.0 %copy.19 = bf16[1,1,128,2560]{3,2,1,0:T(8,128)(2,1)} copy(bf16[1,1,128,2560]{3,2,1,0:T(8,128)(2,1)} %bitcast.13) | data formatting | bytes 1310720
  38.8 1.7 %copy.20 = f32[1,320,256]{2,1,0:T(8,128)} copy(f32[1,320,256]{2,1,0:T(8,128)} %bitcast.17) | data formatting | bytes 655360
  40.6 1.4 %copy.21 = f32[1,50,256]{2,0,1:T(1,128)} copy(f32[1,50,256]{2,0,1:T(1,128)} %bitcast.19) | data formatting | bytes 102400
  42.0 1.2 %copy.22 = f32[1,256]{1,0:T(1,128)} copy(f32[1,256]{1,0:T(1,128)} %get-tuple-element.19) | data formatting | bytes 2048

commit v3 on v2

--- a/solution.py
+++ b/solution.py
@@ -513,6 +513,33 @@
     put_out.wait()
 
 
+def put_kernel(*refs):
+    count = (len(refs) - 2) // 3
+    sources, targets, held = refs[:count], refs[count : 2 * count], refs[2 * count : 3 * count]
+    take_sems, put_sems = refs[-2:]
+    parts = [
+        (i, pl.ds(c * (sources[i].shape[0] // cuts), sources[i].shape[0] // cuts))
+        for i in range(count)
+        for cuts in [2 if i == 0 else 1]
+        for c in range(cuts)
+    ]
+    takes = [
+        pltpu.make_async_copy(sources[i].at[part], held[i].at[part], take_sems.at[s])
+        for s, (i, part) in enumerate(parts)
+    ]
+    puts = [
+        pltpu.make_async_copy(held[i].at[part], targets[i].at[part], put_sems.at[s])
+        for s, (i, part) in enumerate(parts)
+    ]
+    for take in takes:
+        take.start()
+    for take, put in zip(takes, puts):
+        take.wait()
+        put.start()
+    for put in puts:
+        put.wait()
+
+
 def body(
     n,
     n_dp,
@@ -535,14 +562,15 @@
     hbm = pl.BlockSpec(memory_space=pl.ANY)
     smem = pl.BlockSpec(memory_space=pltpu.SMEM)
     dma = pltpu.SemaphoreType.DMA
+    shapes = (
+        jax.ShapeDtypeStruct((toks, dim), BF16),
+        jax.ShapeDtypeStruct((cols_n, rh), F32),
+        jax.ShapeDtypeStruct((steps, 1, rh), F32),
+        jax.ShapeDtypeStruct((1, rh), F32),
+    )
     outs = pl.pallas_call(
         functools.partial(kernel, n, n_dp),
-        out_shape=(
-            jax.ShapeDtypeStruct((toks, dim), BF16),
-            jax.ShapeDtypeStruct((cols_n, rh), F32),
-            jax.ShapeDtypeStruct((steps, 1, rh), F32),
-            jax.ShapeDtypeStruct((1, rh), F32),
-        ),
+        out_shape=shapes,
         in_specs=[hbm, hbm, hbm, smem] + [hbm] * 6,
         out_specs=(hbm,) * 4,
         scratch_shapes=[
@@ -615,7 +643,15 @@
         router_out,
         out_cotangent[0],
     )
-    blended, in_grad, bias_grad, out_grad = outs
+    blended, in_grad, bias_grad, out_grad = pl.pallas_call(
+        put_kernel,
+        out_shape=shapes,
+        in_specs=[hbm] * 4,
+        out_specs=(hbm,) * 4,
+        scratch_shapes=[pltpu.VMEM(shape.shape, shape.dtype) for shape in shapes]
+        + [dma((5,)), dma((5,))],
+        compiler_params=pltpu.CompilerParams(vmem_limit_bytes=67043328),
+    )(*outs)
     return (blended[None, None], in_grad[None], jnp.transpose(bias_grad, (1, 0, 2)), out_grad)
 
 

time: 43.5 us -> 39 us (0.90)
  local copies, waits for them, and re-layouts: 6.35 us -> 0 us
  Pallas kernels: 35.6 us -> 37.6 us
    unnamed x4 -> x0, local copies, waits for them, and re-layouts: 6.35 us -> none
    pallas_call x1 -> x2, Pallas kernels: 35.6 us -> 37.6 us  [the longest x1 35.6 us: body(): pl.pallas_call(functools.partial(kernel, n, n_dp), out_shape=shapes, in_s...]
where the time goes in v3:
time: 39 us; the launch traced here: 38.9 us
  Pallas kernels  37.6 us (96%)
  between operations  1.29 us (3%)
    pallas_call x1, Pallas kernels, body(): pl.pallas_call(functools.partial(kernel, n, n_dp), out_shape=shapes, in_s...  35.6 us
    pallas_call x1, Pallas kernels, body(): pl.pallas_call(put_kernel, out_shape=shapes, in_specs=[hbm] * 4, out_spec...  2.01 us

profile of v3, /device:TPU:0, one launch (start us, length us, event | category | flops | bytes accessed | tf_op | source)
XLA Modules:
  0.0 38.9 jit_solution(9139940906520966021)
XLA Ops:
  1.3 35.6 %shard_map.129 = (bf16[128,2560]{1,0:T(8,128)(2,1)}, f32[320,256]{1,0:T(8,128)}, f32[50,1,256]{2,1,0:T(1,128)}, f32[1,256]{1,0:T(1,128)}) custom-call(bf16[128,2560]{1,0:T(8,128)(2,1)} %bitcast.13, bf16[128,2560]{1,0:T(8,128)(2,1)} %bitcast.14, s32[1,128]{1,0:T(1,128)} %bitcast.18, s32[1]{0:T(128)S(6)} %copy.14.step_ref, bf16[896,2560]{1,0:T(8,128)(2,1)} %bitcast.11, ...), custom_call_target="tpu_custom_call" | custom-call | tf_op jit(solution)/shard_map/pallas_call | solution.py:571
  36.9 2.0 %shard_map.130 = (bf16[128,2560]{1,0:T(8,128)(2,1)}, f32[320,256]{1,0:T(8,128)}, f32[50,1,256]{2,1,0:T(1,128)}, f32[1,256]{1,0:T(1,128)}) custom-call(bf16[128,2560]{1,0:T(8,128)(2,1)} %get-tuple-element.12.refs_0_, f32[320,256]{1,0:T(8,128)} %get-tuple-element.13.refs_1_, f32[50,1,256]{2,1,0:T(1,128)} %get-tuple-element.14.refs_2_, ...), custom_call_target="tpu_custom_call" | custom-call | tf_op jit(solution)/shard_map/pallas_call | solution.py:646

commit v4 on v3

--- a/solution.py
+++ b/solution.py
@@ -133,6 +133,13 @@
     rh = rin_ref.shape[1]
     cols_n = rin_ref.shape[0]
     rows = n * FRESH
+    toward = 2 * ((2 * k) // n) - 1
+
+    def ring(i):
+        return lax.rem(k + n + toward * i, n)
+
+    def ring_all(i):
+        return ring(i // n_dp + 1), lax.rem(v + 1 + lax.rem(i, n_dp), n_dp)
 
     load_mask = pltpu.make_async_copy(mask_hbm, mask_ref, load_sem.at[0])
     load_rows = pltpu.make_async_copy(tokens_hbm, first, load_sem.at[1])
@@ -217,14 +224,14 @@
     def _():
         @pl.loop(1, n)
         def _(i):
-            j = lax.rem(k + i, n)
+            j = ring(i)
             peer_copy(xin.at[k], xin.at[k], x_send.at[j], x_recv.at[k], j).start()
 
     @pl.when(is1)
     def _():
         @pl.loop(1, n)
         def _(i):
-            j = lax.rem(k + i, n)
+            j = ring(i)
             peer_copy(cin.at[k], cin.at[k], x_send.at[j], c_recv.at[k], j).start()
 
     sel_copy = peer_copy(sel, psel, sel_sems.at[0], sel_sems.at[1], k, pipe=1 - p)
@@ -285,7 +292,7 @@
 
     @pl.loop(1, n)
     def _(i):
-        j = lax.rem(k + i, n)
+        j = ring(i)
         peer_copy(send1.at[j], recv1.at[k], r1_send.at[j], r1_recv.at[k], j).start()
 
     @pl.when(is1)
@@ -312,7 +319,7 @@
 
         @pl.loop(1, n)
         def _(i):
-            j = lax.rem(k + i, n)
+            j = ring(i)
             peer_copy(send2.at[j], recv2.at[k], r2_send.at[j], r2_recv.at[k], j).start()
 
         recv2[k] = send2[k]
@@ -368,7 +375,7 @@
 
         @pl.loop(0, n)
         def _(i):
-            j = lax.rem(k + i, n)
+            j = ring(i + 1)
             peer_copy(in1, xin.at[k], f_send.at[j], x_recv.at[k], j, pipe=1).start()
 
         met = same_0 * gap[0:1] + same_1 * gap[1:2]
@@ -376,8 +383,12 @@
         w1[...] = normalize_back(scaled, inv_std, met).astype(BF16)
 
         @pl.loop(0, n)
-        def _(i):
-            j = lax.rem(k + i, n)
+        def _(j):
+            peer_copy(in1, xin.at[j], f_send.at[j], x_recv.at[j], j, pipe=1).wait_send()
+
+        @pl.loop(0, n)
+        def _(i):
+            j = ring(i + 1)
             peer_copy(w1, win.at[k], w_send.at[j], w_recv.at[k], j, pipe=1).start()
 
         delta[...] = met
@@ -389,7 +400,6 @@
 
         @pl.loop(0, n)
         def _(j):
-            peer_copy(in1, xin.at[j], f_send.at[j], x_recv.at[j], j, pipe=1).wait_send()
             peer_copy(w1, win.at[j], w_send.at[j], w_recv.at[j], j, pipe=1).wait_send()
 
         delta_copy.wait_send()
@@ -410,13 +420,6 @@
     def _():
         gate_grad = jnp.sum(picked * gap, axis=1, keepdims=True)
         message(gmsg.at[slot], gate_grad, hid_factor, out_factor)
-
-        @pl.loop(1, n * n_dp)
-        def _(i):
-            t = lax.rem(slot + i, n * n_dp)
-            peer_copy(
-                gmsg.at[slot], gmsg.at[slot], g_send.at[t], g_recv.at[slot], lax.rem(t, n), dp=t // n
-            ).start()
 
         delta_copy.wait_recv()
         factor_copy.wait_recv()
@@ -443,15 +446,22 @@
 
         @pl.loop(0, n * n_dp)
         def _(i):
-            t = lax.rem(slot + i, n * n_dp)
+            j, u = ring_all(i)
             peer_copy(
                 gfirst,
                 gmsg.at[slot],
-                g_send.at[n * n_dp + t],
+                g_send.at[n * n_dp + u * n + j],
                 g_recv.at[slot],
-                lax.rem(t, n),
+                j,
                 pipe=0,
-                dp=t // n,
+                dp=u,
+            ).start()
+
+        @pl.loop(0, n * n_dp - 1)
+        def _(i):
+            j, u = ring_all(i)
+            peer_copy(
+                gmsg.at[slot], gmsg.at[slot], g_send.at[u * n + j], g_recv.at[slot], j, dp=u
             ).start()
 
         blend_out()

time: 39 us -> 38.2 us (0.979)
  Pallas kernels: 37.6 us -> 36.8 us
    pallas_call x1, Pallas kernels: 35.6 us -> 34.8 us  [body(): pl.pallas_call(functools.partial(kernel, n, n_dp), out_shape=shapes, in_s...]
where the time goes in v4:
time: 38.2 us; the launch traced here: 38.1 us
  Pallas kernels  36.8 us (96%)
  between operations  1.29 us (3%)
    pallas_call x1, Pallas kernels, body(): pl.pallas_call(functools.partial(kernel, n, n_dp), out_shape=shapes, in_s...  34.8 us
    pallas_call x1, Pallas kernels, body(): pl.pallas_call(put_kernel, out_shape=shapes, in_specs=[hbm] * 4, out_spec...  2.01 us

profile of v4, /device:TPU:0, one launch (start us, length us, event | category | flops | bytes accessed | tf_op | source)
XLA Modules:
  0.0 38.1 jit_solution(3205703173264502051)
XLA Ops:
  1.3 34.8 %shard_map.129 = (bf16[128,2560]{1,0:T(8,128)(2,1)}, f32[320,256]{1,0:T(8,128)}, f32[50,1,256]{2,1,0:T(1,128)}, f32[1,256]{1,0:T(1,128)}) custom-call(bf16[128,2560]{1,0:T(8,128)(2,1)} %bitcast.13, bf16[128,2560]{1,0:T(8,128)(2,1)} %bitcast.14, s32[1,128]{1,0:T(1,128)} %bitcast.18, s32[1]{0:T(128)S(6)} %copy.14.step_ref, bf16[896,2560]{1,0:T(8,128)(2,1)} %bitcast.11, ...), custom_call_target="tpu_custom_call" | custom-call | tf_op jit(solution)/shard_map/pallas_call | solution.py:581
  36.1 2.0 %shard_map.130 = (bf16[128,2560]{1,0:T(8,128)(2,1)}, f32[320,256]{1,0:T(8,128)}, f32[50,1,256]{2,1,0:T(1,128)}, f32[1,256]{1,0:T(1,128)}) custom-call(bf16[128,2560]{1,0:T(8,128)(2,1)} %get-tuple-element.12.refs_0_, f32[320,256]{1,0:T(8,128)} %get-tuple-element.13.refs_1_, f32[50,1,256]{2,1,0:T(1,128)} %get-tuple-element.14.refs_2_, ...), custom_call_target="tpu_custom_call" | custom-call | tf_op jit(solution)/shard_map/pallas_call | solution.py:656
